TPU v7x, 32 devices: a whole 2x2x4 slice. The times are simulated.
32 devices in a mesh: gz: 8 (over z, y), xy: 4 (over x, core).
Axes of the slice: x: 2, y: 2, z: 4, core: 2. Of those that a mesh axis runs over, the one named last changes fastest.
Arguments:
- up_source: bfloat16 [8, 2, 32, 1024], P('gz', None, None, 'xy'), may hold values from -6 to 6
- down_source: bfloat16 [8, 2, 32, 1024], P('gz', None, None, 'xy'), may hold values from -6 to 6
- source_layer: int32 [32], replicated, may hold values from 0 to 7, as said below
- u_factor: bfloat16 [8, 4, 4, 2, 128, 256], P('gz', 'xy'), may hold values from -0.15625 to 0.15625
- v_factor: bfloat16 [8, 4, 4, 2, 128, 256], P('gz', 'xy'), may hold values from -0.25 to 0.25
- block_rank: int32 [8, 4, 4], P('gz', 'xy'), may hold values from 1 to 4
Outputs:
- up_trace: bfloat16 [8, 2, 32, 1024], P('gz', None, None, 'xy')
- down_trace: bfloat16 [8, 2, 32, 1024], P('gz', None, None, 'xy')
Inputs may be any that keep to these rules, and one draw needn't show every extreme that they name: `source_layer`: the index of the layer slab in which source s lies; source 0 lies in slab 0 and source 1 in slab 8 - 1. `block_rank`: block (i, j) of interface l has rank 32 times this number.
All inputs are finite; a program needn't handle non-finite values.
Results may differ from a plain program's by a relative error of at most 0.007.
Values may be sent and summed in bfloat16 or wider, within the bound.
A program may use at most 64 MiB of HBM per device.

v0:
```python
import jax
import jax.numpy as jnp
from jax import lax
from jax.sharding import PartitionSpec as P

STEPS = 3


def from_behind(block, axis, distance):
    devices = range(lax.axis_size(axis))
    route = [(i - distance, i) for i in devices if i - distance in devices]
    return lax.ppermute(block, axis, route)


def complex_parts(product):
    real = product[..., 0, :, 0, :] - product[..., 1, :, 1, :]
    imag = product[..., 0, :, 1, :] + product[..., 1, :, 0, :]
    return jnp.stack([real, imag], axis=-3)


def advance(up_part, down_part, active_up, active_down, u_layer, v_layer, keep_rank, v_columns):
    sources = up_part.shape[1]
    own_rows = u_layer.shape[0]
    blocks = u_layer.shape[1]
    width = u_layer.shape[-1]
    gathered = lax.all_gather(up_part, "xy", axis=2, tiled=True)
    pieces = gathered.reshape(2, sources, blocks, width)
    up_coef = complex_parts(
        jnp.einsum("asjb,ijcrb->ijascr", pieces, v_layer, preferred_element_type=jnp.float32)
    )
    up_coef = jnp.where(keep_rank[:, :, None, None, :], up_coef, 0.0).astype(jnp.bfloat16)
    forward = complex_parts(
        jnp.einsum("ijasr,ijcrb->iascb", up_coef, u_layer, preferred_element_type=jnp.float32)
    )
    forward = jnp.transpose(forward, (1, 2, 0, 3)).reshape(2, sources, own_rows * width)
    arrived = from_behind(forward, "gz", 1)
    new_up = (active_up.astype(jnp.float32) + arrived).astype(jnp.bfloat16)
    upper = from_behind(down_part, "gz", -1)
    upper_blocks = upper.reshape(2, sources, own_rows, width)
    down_coef = complex_parts(
        jnp.einsum("asib,ijcrb->ijascr", upper_blocks, u_layer, preferred_element_type=jnp.float32)
    )
    down_coef = jnp.where(keep_rank[:, :, None, None, :], down_coef, 0.0).astype(jnp.bfloat16)
    column_coef = lax.all_to_all(down_coef, "xy", split_axis=1, concat_axis=0, tiled=True)
    summed = complex_parts(
        jnp.einsum("ijasr,ijcrb->jascb", column_coef, v_columns, preferred_element_type=jnp.float32)
    )
    backward = jnp.transpose(summed, (1, 2, 0, 3)).reshape(2, sources, own_rows * width)
    new_down = (active_down.astype(jnp.float32) + backward).astype(jnp.bfloat16)
    return (new_up, new_down)


def on_device(up_source, down_source, source_layer, u_factor, v_factor, block_rank):
    layer_index = lax.axis_index("gz")
    up_mask = (layer_index >= source_layer)[None, :, None]
    down_mask = (layer_index <= source_layer)[None, :, None]
    active_up = jnp.where(up_mask, up_source[0], jnp.zeros_like(up_source[0]))
    active_down = jnp.where(down_mask, down_source[0], jnp.zeros_like(down_source[0]))
    u_layer = u_factor[0]
    v_layer = v_factor[0]
    rank_units = block_rank[0]
    max_rank = u_layer.shape[-2]
    keep_rank = (
        jnp.arange(max_rank, dtype=jnp.int32)[None, None, :]
        < max_rank // 4 * rank_units[:, :, None]
    )
    v_columns = lax.all_to_all(v_layer, "xy", split_axis=1, concat_axis=0, tiled=True)
    up_trace = active_up
    down_trace = active_down
    for sweep_index in range(STEPS):
        up_trace, down_trace = advance(
            up_trace, down_trace, active_up, active_down, u_layer, v_layer, keep_rank, v_columns
        )
    return (up_trace[None], down_trace[None])


def solution(mesh):
    in_specs = (
        P("gz", None, None, "xy"),
        P("gz", None, None, "xy"),
        P(),
        P("gz", "xy", None, None, None, None),
        P("gz", "xy", None, None, None, None),
        P("gz", "xy", None),
    )
    out_specs = (P("gz", None, None, "xy"), P("gz", None, None, "xy"))
    return jax.shard_map(
        on_device, mesh=mesh, in_specs=in_specs, out_specs=out_specs, check_vma=False
    )
```

profile of v0, /device:TPU:0, one launch (start us, length us, event | category | flops | bytes accessed | tf_op | source)
XLA Modules:
  0.0 86.9 jit_solution(7317015157043258093)
XLA Ops:
  0.6 0.0 copy-start
  0.6 0.0 copy-start.3
  0.7 0.7 copy-done.3
  1.4 0.0 copy-start.1
  1.4 0.8 bitcast_select_fusion
  2.2 1.3 %collective-permute-start.3 = (bf16[2,32,256]{2,1,0:T(8,128)(2,1)S(1)}, bf16[2,32,256]{2,1,0:T(8,128)(2,1)S(1)}, u32[]{:S(2)}, u32[]{:S(2)}) collective-permute-start(bf16[2,32,256]{2,1,0:T(8,128)(2,1)S(1)} %bitcast_select_fusion), channel_id=1, source_target_pairs={{4,0},{8,4},{12,8},{16,12},{20,16},{24,20},{28,24},{5,1},{9,5},{13... | collective-permute-start | bytes 98312 | tf_op jit(solution)/shard_map/ppermute | solution.py:12
  3.5 0.0 copy-done.1
  3.5 0.1 bitcast_select_fusion.1
  3.6 6.5 %all_gather.9 = bf16[2,32,1024]{2,1,0:T(8,128)(2,1)S(1)} all-gather(bf16[2,32,256]{2,1,0:T(8,128)(2,1)S(1)} %bitcast_select_fusion.1), channel_id=1, replica_groups=mesh['gz'=8,'xy'=4] {'xy'}, dimensions={2}, use_global_device_ids=true | all-gather | bytes 163840 | tf_op jit(solution)/shard_map/all_gather | solution.py:26
  10.1 0.1 reshape.884
  10.2 1.3 %convolution_bitcast_fusion.5 = f32[1,4,2,32,2,128]{5,3,4,2,1,0:T(8,128)S(1)} fusion(bf16[1,1,4,2,128,256]{5,4,3,2,1,0:T(8,128)(2,1)} %param.10, bf16[2,32,4,256,1]{3,2,1,0,4:T(4,128)(2,1)S(1)} %bitcast.274), kind=kOutput, calls=%fused_computation.5 | convolution fusion | flops 33554432 | bytes 917504 | tf_op jit(solution)/shard_map/asjb,ijcrb->ijascr/dot_general | solution.py:29
  11.5 0.0 copy-start.4
  11.5 0.6 copy-done.4
  12.2 0.1 iota_compare_fusion
  12.2 0.0 copy-done
  12.2 0.2 convolution_bitcast_fusion.11
  12.5 4.5 %collective-permute-start = (f32[2,32,256]{2,1,0:T(8,128)S(1)}, f32[2,32,256]{2,1,0:T(8,128)S(1)}, u32[]{:S(2)}, u32[]{:S(2)}) collective-permute-start(f32[2,32,256]{2,1,0:T(8,128)S(1)} %maximum_bitcast_fusion), channel_id=1, source_target_pairs={{0,4},{4,8},{8,12},{12,16},{16,20},{20,24},{24,28},{1,5},{5,9},{9,... | collective-permute-start | bytes 196616 | tf_op jit(solution)/shard_map/ppermute | solution.py:12
  17.0 0.0 collective-permute-done.3
  17.1 0.3 convolution_bitcast_fusion.2
  17.4 1.6 %collective-permute-done = f32[2,32,256]{2,1,0:T(8,128)S(1)} collective-permute-done((f32[2,32,256]{2,1,0:T(8,128)S(1)}, f32[2,32,256]{2,1,0:T(8,128)S(1)}, u32[]{:S(2)}, u32[]{:S(2)}) %collective-permute-start) | collective-permute-done | bytes 65568 | tf_op jit(solution)/shard_map/ppermute | solution.py:12
  18.9 0.1 fusion.33
  19.0 5.4 %all_gather.10 = bf16[2,32,1024]{2,1,0:T(8,128)(2,1)S(1)} all-gather(bf16[2,32,256]{2,1,0:T(8,128)(2,1)S(1)} %fusion.33), channel_id=1, replica_groups=mesh['gz'=8,'xy'=4] {'xy'}, dimensions={2}, use_global_device_ids=true | all-gather | bytes 163840 | tf_op jit(solution)/shard_map/all_gather | solution.py:26
  24.4 0.1 reshape.887
  24.5 1.3 %convolution_bitcast_fusion.4 = f32[1,4,2,32,2,128]{5,3,1,4,2,0:T(8,128)S(1)} fusion(bf16[2,32,4,256,1]{3,2,1,0,4:T(4,128)(2,1)S(1)} %bitcast.275, bf16[1,1,4,2,128,256]{5,4,3,2,1,0:T(8,128)(2,1)} %param.10), kind=kOutput, calls=%fused_computation.4 | convolution fusion | flops 33554432 | bytes 917504 | tf_op jit(solution)/shard_map/asjb,ijcrb->ijascr/dot_general | solution.py:29
  25.8 0.2 convolution_bitcast_fusion.10
  26.1 4.7 %collective-permute-start.1 = (f32[2,32,256]{2,1,0:T(8,128)S(1)}, f32[2,32,256]{2,1,0:T(8,128)S(1)}, u32[]{:S(2)}, u32[]{:S(2)}) collective-permute-start(f32[2,32,256]{2,1,0:T(8,128)S(1)} %maximum_bitcast_fusion.1), channel_id=1, source_target_pairs={{0,4},{4,8},{8,12},{12,16},{16,20},{20,24},{24,28},{1,5},{5,9},{9,... | collective-permute-start | bytes 196616 | tf_op jit(solution)/shard_map/ppermute | solution.py:12
  30.8 0.6 copy.49
  31.4 3.3 %all-to-all-start = ((bf16[1,4,2,32,128]{4,3,2,0,1:T(8,128)(2,1)}), bf16[1,4,2,32,128]{4,3,2,0,1:T(8,128)(2,1)S(1)}, u32[]{:S(2)}, u32[]{:S(2)}) async-start(bf16[1,4,2,32,128]{4,3,2,0,1:T(8,128)(2,1)} %copy.49), calls=%async_computation | async-start | bytes 131072 | tf_op jit(solution)/shard_map/all_to_all | solution.py:44
  34.7 0.0 collective-permute-done.1
  34.7 0.1 fusion.34
  34.8 4.0 %all-to-all-done = bf16[1,4,2,32,128]{4,3,2,0,1:T(8,128)(2,1)S(1)} async-done(((bf16[1,4,2,32,128]{4,3,2,0,1:T(8,128)(2,1)}), bf16[1,4,2,32,128]{4,3,2,0,1:T(8,128)(2,1)S(1)}, u32[]{:S(2)}, u32[]{:S(2)}) %all-to-all-start) | async-done | bytes 65568 | tf_op jit(solution)/shard_map/all_to_all | solution.py:44
  38.8 3.5 %all-to-all-start.1 = ((bf16[1,4,2,128,256]{4,3,2,0,1:T(8,128)(2,1)}), bf16[1,4,2,128,256]{4,3,2,0,1:T(8,128)(2,1)S(1)}, u32[]{:S(2)}, u32[]{:S(2)}) async-start(bf16[1,4,2,128,256]{4,3,2,0,1:T(8,128)(2,1)} %bitcast.74), calls=%async_computation.1 | async-start | bytes 1048576 | tf_op jit(solution)/shard_map/all_to_all | solution.py:67
  42.3 10.3 %all_gather.11 = bf16[2,32,1024]{2,1,0:T(8,128)(2,1)S(1)} all-gather(bf16[2,32,256]{2,1,0:T(8,128)(2,1)S(1)} %fusion.34), channel_id=1, replica_groups=mesh['gz'=8,'xy'=4] {'xy'}, dimensions={2}, use_global_device_ids=true | all-gather | bytes 163840 | tf_op jit(solution)/shard_map/all_gather | solution.py:26
  52.6 0.1 reshape.888
  52.7 1.3 %convolution_bitcast_fusion.3 = f32[1,4,2,32,2,128]{5,3,1,4,2,0:T(8,128)S(1)} fusion(bf16[2,32,4,256,1]{3,2,1,0,4:T(4,128)(2,1)S(1)} %bitcast.276, bf16[1,1,4,2,128,256]{5,4,3,2,1,0:T(8,128)(2,1)} %param.10), kind=kOutput, calls=%fused_computation.3 | convolution fusion | flops 33554432 | bytes 917504 | tf_op jit(solution)/shard_map/asjb,ijcrb->ijascr/dot_general | solution.py:29
  54.0 0.0 all-to-all-done.1
  54.1 0.2 convolution_bitcast_fusion.8
  54.3 0.0 copy-start.2
  54.3 0.7 copy-done.2
  55.0 0.1 fusion.31
  55.1 1.3 %collective-permute-start.4 = (bf16[2,32,256]{2,1,0:T(8,128)(2,1)S(1)}, bf16[2,32,256]{2,1,0:T(8,128)(2,1)S(1)}, u32[]{:S(2)}, u32[]{:S(2)}) collective-permute-start(bf16[2,32,256]{2,1,0:T(8,128)(2,1)S(1)} %fusion.31), channel_id=1, source_target_pairs={{4,0},{8,4},{12,8},{16,12},{20,16},{24,20},{28,24},{5,1},{9,5},{13... | collective-permute-start | bytes 98312 | tf_op jit(solution)/shard_map/ppermute | solution.py:12
  56.4 0.2 convolution_bitcast_fusion.9
  56.6 5.6 %collective-permute-done.4 = bf16[2,32,256]{2,1,0:T(8,128)(2,1)S(1)} collective-permute-done((bf16[2,32,256]{2,1,0:T(8,128)(2,1)S(1)}, bf16[2,32,256]{2,1,0:T(8,128)(2,1)S(1)}, u32[]{:S(2)}, u32[]{:S(2)}) %collective-permute-start.4) | collective-permute-done | bytes 32800 | tf_op jit(solution)/shard_map/ppermute | solution.py:12
  62.2 0.3 convolution_bitcast_fusion.1
  62.6 0.6 copy.53
  63.2 3.3 %all-to-all-start.2 = ((bf16[1,4,2,32,128]{4,3,2,0,1:T(8,128)(2,1)}), bf16[1,4,2,32,128]{4,3,2,0,1:T(8,128)(2,1)S(1)}, u32[]{:S(2)}, u32[]{:S(2)}) async-start(bf16[1,4,2,32,128]{4,3,2,0,1:T(8,128)(2,1)} %copy.53), calls=%async_computation.2 | async-start | bytes 131072 | tf_op jit(solution)/shard_map/all_to_all | solution.py:44
  66.5 4.1 %all-to-all-done.2 = bf16[1,4,2,32,128]{4,3,2,0,1:T(8,128)(2,1)S(1)} async-done(((bf16[1,4,2,32,128]{4,3,2,0,1:T(8,128)(2,1)}), bf16[1,4,2,32,128]{4,3,2,0,1:T(8,128)(2,1)S(1)}, u32[]{:S(2)}, u32[]{:S(2)}) %all-to-all-start.2) | async-done | bytes 65568 | tf_op jit(solution)/shard_map/all_to_all | solution.py:44
  70.6 0.2 convolution_bitcast_fusion.7
  70.8 0.1 fusion.32
  70.9 1.3 %collective-permute-start.5 = (bf16[2,32,256]{2,1,0:T(8,128)(2,1)S(1)}, bf16[2,32,256]{2,1,0:T(8,128)(2,1)S(1)}, u32[]{:S(2)}, u32[]{:S(2)}) collective-permute-start(bf16[2,32,256]{2,1,0:T(8,128)(2,1)S(1)} %fusion.32), channel_id=1, source_target_pairs={{4,0},{8,4},{12,8},{16,12},{20,16},{24,20},{28,24},{5,1},{9,5},{13... | collective-permute-start | bytes 98312 | tf_op jit(solution)/shard_map/ppermute | solution.py:12
  72.2 5.5 %collective-permute-start.2 = (f32[2,32,256]{2,1,0:T(8,128)S(1)}, f32[2,32,256]{2,1,0:T(8,128)S(1)}, u32[]{:S(2)}, u32[]{:S(2)}) collective-permute-start(f32[2,32,256]{2,1,0:T(8,128)S(1)} %maximum_bitcast_fusion.2), channel_id=1, source_target_pairs={{0,4},{4,8},{8,12},{12,16},{16,20},{20,24},{24,28},{1,5},{5,9},{9,... | collective-permute-start | bytes 196616 | tf_op jit(solution)/shard_map/ppermute | solution.py:12
  77.6 0.0 collective-permute-done.5
  77.6 0.3 convolution_bitcast_fusion
  78.0 0.6 copy.56
  78.6 3.3 %all-to-all-start.3 = ((bf16[1,4,2,32,128]{4,3,2,0,1:T(8,128)(2,1)}), bf16[1,4,2,32,128]{4,3,2,0,1:T(8,128)(2,1)S(1)}, u32[]{:S(2)}, u32[]{:S(2)}) async-start(bf16[1,4,2,32,128]{4,3,2,0,1:T(8,128)(2,1)} %copy.56), calls=%async_computation.3 | async-start | bytes 131072 | tf_op jit(solution)/shard_map/all_to_all | solution.py:44
  81.9 0.0 collective-permute-done.2
  81.9 0.7 fusion.69
  82.6 3.4 %all-to-all-done.3 = bf16[1,4,2,32,128]{4,3,2,0,1:T(8,128)(2,1)S(1)} async-done(((bf16[1,4,2,32,128]{4,3,2,0,1:T(8,128)(2,1)}), bf16[1,4,2,32,128]{4,3,2,0,1:T(8,128)(2,1)S(1)}, u32[]{:S(2)}, u32[]{:S(2)}) %all-to-all-start.3) | async-done | bytes 65568 | tf_op jit(solution)/shard_map/all_to_all | solution.py:44
  86.0 0.2 convolution_bitcast_fusion.6
  86.2 0.7 fusion.56
  (22 shorter events, 0.3 us)
Async XLA Ops:
  0.6 11.6 %copy-start = (bf16[1,1,4,2,128,256]{5,4,3,2,1,0:T(8,128)(2,1)S(1)}, bf16[1,1,4,2,128,256]{5,4,3,2,1,0:T(8,128)(2,1)}, u32[]{:S(2)}) copy-start(bf16[1,1,4,2,128,256]{5,4,3,2,1,0:T(8,128)(2,1)} %param.9) | copy-start | bytes 1572868
  0.6 0.7 copy-start.3
  1.4 2.1 %copy-start.1 = (bf16[1,2,32,256]{3,2,1,0:T(8,128)(2,1)S(1)}, bf16[1,2,32,256]{3,2,1,0:T(8,128)(2,1)}, u32[]{:S(2)}) copy-start(bf16[1,2,32,256]{3,2,1,0:T(8,128)(2,1)} %param.6) | copy-start | bytes 98308
  2.2 14.8 %collective-permute-start.3 = (bf16[2,32,256]{2,1,0:T(8,128)(2,1)S(1)}, bf16[2,32,256]{2,1,0:T(8,128)(2,1)S(1)}, u32[]{:S(2)}, u32[]{:S(2)}) collective-permute-start(bf16[2,32,256]{2,1,0:T(8,128)(2,1)S(1)} %bitcast_select_fusion), channel_id=1, source_target_pairs={{4,0},{8,4},{12,8},{16,12},{20,16},{24,20},{28,24},{5,1},{9,5},{13... | collective-permute-start | bytes 98312 | tf_op jit(solution)/shard_map/ppermute | solution.py:12
  11.5 0.7 copy-start.4
  12.5 6.4 %collective-permute-start = (f32[2,32,256]{2,1,0:T(8,128)S(1)}, f32[2,32,256]{2,1,0:T(8,128)S(1)}, u32[]{:S(2)}, u32[]{:S(2)}) collective-permute-start(f32[2,32,256]{2,1,0:T(8,128)S(1)} %maximum_bitcast_fusion), channel_id=1, source_target_pairs={{0,4},{4,8},{8,12},{12,16},{16,20},{20,24},{24,28},{1,5},{5,9},{9,... | collective-permute-start | bytes 196616 | tf_op jit(solution)/shard_map/ppermute | solution.py:12
  26.1 8.7 %collective-permute-start.1 = (f32[2,32,256]{2,1,0:T(8,128)S(1)}, f32[2,32,256]{2,1,0:T(8,128)S(1)}, u32[]{:S(2)}, u32[]{:S(2)}) collective-permute-start(f32[2,32,256]{2,1,0:T(8,128)S(1)} %maximum_bitcast_fusion.1), channel_id=1, source_target_pairs={{0,4},{4,8},{8,12},{12,16},{16,20},{20,24},{24,28},{1,5},{5,9},{9,... | collective-permute-start | bytes 196616 | tf_op jit(solution)/shard_map/ppermute | solution.py:12
  31.4 7.4 %all-to-all-start = ((bf16[1,4,2,32,128]{4,3,2,0,1:T(8,128)(2,1)}), bf16[1,4,2,32,128]{4,3,2,0,1:T(8,128)(2,1)S(1)}, u32[]{:S(2)}, u32[]{:S(2)}) async-start(bf16[1,4,2,32,128]{4,3,2,0,1:T(8,128)(2,1)} %copy.49), calls=%async_computation | async-start | bytes 131072 | tf_op jit(solution)/shard_map/all_to_all | solution.py:44
  38.8 15.2 %all-to-all-start.1 = ((bf16[1,4,2,128,256]{4,3,2,0,1:T(8,128)(2,1)}), bf16[1,4,2,128,256]{4,3,2,0,1:T(8,128)(2,1)S(1)}, u32[]{:S(2)}, u32[]{:S(2)}) async-start(bf16[1,4,2,128,256]{4,3,2,0,1:T(8,128)(2,1)} %bitcast.74), calls=%async_computation.1 | async-start | bytes 1048576 | tf_op jit(solution)/shard_map/all_to_all | solution.py:67
  54.3 0.8 copy-start.2
  55.1 7.1 %collective-permute-start.4 = (bf16[2,32,256]{2,1,0:T(8,128)(2,1)S(1)}, bf16[2,32,256]{2,1,0:T(8,128)(2,1)S(1)}, u32[]{:S(2)}, u32[]{:S(2)}) collective-permute-start(bf16[2,32,256]{2,1,0:T(8,128)(2,1)S(1)} %fusion.31), channel_id=1, source_target_pairs={{4,0},{8,4},{12,8},{16,12},{20,16},{24,20},{28,24},{5,1},{9,5},{13... | collective-permute-start | bytes 98312 | tf_op jit(solution)/shard_map/ppermute | solution.py:12
  63.2 7.4 %all-to-all-start.2 = ((bf16[1,4,2,32,128]{4,3,2,0,1:T(8,128)(2,1)}), bf16[1,4,2,32,128]{4,3,2,0,1:T(8,128)(2,1)S(1)}, u32[]{:S(2)}, u32[]{:S(2)}) async-start(bf16[1,4,2,32,128]{4,3,2,0,1:T(8,128)(2,1)} %copy.53), calls=%async_computation.2 | async-start | bytes 131072 | tf_op jit(solution)/shard_map/all_to_all | solution.py:44
  70.9 6.8 %collective-permute-start.5 = (bf16[2,32,256]{2,1,0:T(8,128)(2,1)S(1)}, bf16[2,32,256]{2,1,0:T(8,128)(2,1)S(1)}, u32[]{:S(2)}, u32[]{:S(2)}) collective-permute-start(bf16[2,32,256]{2,1,0:T(8,128)(2,1)S(1)} %fusion.32), channel_id=1, source_target_pairs={{4,0},{8,4},{12,8},{16,12},{20,16},{24,20},{28,24},{5,1},{9,5},{13... | collective-permute-start | bytes 98312 | tf_op jit(solution)/shard_map/ppermute | solution.py:12
  72.2 9.7 %collective-permute-start.2 = (f32[2,32,256]{2,1,0:T(8,128)S(1)}, f32[2,32,256]{2,1,0:T(8,128)S(1)}, u32[]{:S(2)}, u32[]{:S(2)}) collective-permute-start(f32[2,32,256]{2,1,0:T(8,128)S(1)} %maximum_bitcast_fusion.2), channel_id=1, source_target_pairs={{0,4},{4,8},{8,12},{12,16},{16,20},{20,24},{24,28},{1,5},{5,9},{9,... | collective-permute-start | bytes 196616 | tf_op jit(solution)/shard_map/ppermute | solution.py:12
  78.6 7.4 %all-to-all-start.3 = ((bf16[1,4,2,32,128]{4,3,2,0,1:T(8,128)(2,1)}), bf16[1,4,2,32,128]{4,3,2,0,1:T(8,128)(2,1)S(1)}, u32[]{:S(2)}, u32[]{:S(2)}) async-start(bf16[1,4,2,32,128]{4,3,2,0,1:T(8,128)(2,1)} %copy.56), calls=%async_computation.3 | async-start | bytes 131072 | tf_op jit(solution)/shard_map/all_to_all | solution.py:44
where the time goes:
time: 87.8 us; the launch traced here: 86.9 us
  starting transfers between devices  31.9 us (36%)
  blocking collectives  22.2 us (25%)
  waiting for transfers between devices  18.6 us (21%)
  matrix products  6 us (7%)
  local copies, waits for them, and re-layouts  4.16 us (5%)
  other arithmetic  3 us (3%)
  between operations  1.02 us (1%)
    all_gather x3, blocking collectives, advance(): gathered = lax.all_gather(up_part, 'xy', axis=2, tiled=True)  22.2 us
    ppermute x6, starting transfers between devices, from_behind(): return lax.ppermute(block, axis, route)  18.5 us
    all_to_all x3, waiting for transfers between devices, advance(): lax.all_to_all(down_coef, 'xy', split_axis=1, concat_axis=0, tiled=True)  11.4 us
    all_to_all x3, starting transfers between devices, advance(): lax.all_to_all(down_coef, 'xy', split_axis=1, concat_axis=0, tiled=True)  9.85 us
    ppermute x6, waiting for transfers between devices, from_behind(): return lax.ppermute(block, axis, route)  7.18 us
    dot_general x3, matrix products, advance(): jnp.einsum('asjb,ijcrb->ijascr', pieces, v_layer, preferred_element_type=...  3.95 us
    all_to_all x1, starting transfers between devices, on_device(): lax.all_to_all(v_layer, 'xy', split_axis=1, concat_axis=0, tiled=True)  3.47 us
    unnamed x10, local copies, waits for them, and re-layouts  2.08 us
  transfers between devices with their start and end apart: 10, of which 5 were waited for; matrix products, arithmetic and copies ran while one was open for 7% of the time, Pallas kernels for 0%

commit v1 on v0

--- a/solution.py
+++ b/solution.py
@@ -4,6 +4,17 @@
 from jax.sharding import PartitionSpec as P
 
 STEPS = 3
+
+
+def gather_by_hops(x, name, dim):
+    count = lax.axis_size(name)
+    hops = [(i, (i + 1) % count) for i in range(count)]
+    parts = [x]
+    for hop in range(1, count):
+        parts = [lax.ppermute(parts[0], name, hops), *parts]
+    whole = jnp.concatenate(parts, axis=dim)
+    shift = (lax.axis_index(name) + 1) * parts[-1].shape[dim]
+    return jnp.roll(whole, shift, axis=dim)
 
 
 def from_behind(block, axis, distance):
@@ -23,7 +34,7 @@
     own_rows = u_layer.shape[0]
     blocks = u_layer.shape[1]
     width = u_layer.shape[-1]
-    gathered = lax.all_gather(up_part, "xy", axis=2, tiled=True)
+    gathered = gather_by_hops(up_part, "xy", 2)
     pieces = gathered.reshape(2, sources, blocks, width)
     up_coef = complex_parts(
         jnp.einsum("asjb,ijcrb->ijascr", pieces, v_layer, preferred_element_type=jnp.float32)

time: 87.8 us -> 81.5 us (0.928)
  blocking collectives: 22.2 us -> 0 us
  waiting for transfers between devices: 18.6 us -> 34.1 us
  local copies, waits for them, and re-layouts: 4.16 us -> 2.85 us
  starting transfers between devices: 31.9 us -> 33 us
    all_gather x3 -> x0, blocking collectives: 22.2 us -> none  [advance(): gathered = lax.all_gather(up_part, 'xy', axis=2, tiled=True)]
    ppermute x0 -> x9, waiting for transfers between devices: none -> 19.8 us  [gather_by_hops(): parts = [lax.ppermute(parts[0], name, hops), *parts]]
    all_to_all x3, waiting for transfers between devices: 11.4 us -> 7.73 us  [advance(): lax.all_to_all(down_coef, 'xy', split_axis=1, concat_axis=0, tiled=True)]
    ppermute x0 -> x9, starting transfers between devices: none -> 1.46 us  [gather_by_hops(): parts = [lax.ppermute(parts[0], name, hops), *parts]]
    unnamed x10, local copies, waits for them, and re-layouts: 2.08 us -> 0.73 us
  transfers between devices with their start and end apart: 10 -> 19, of which waited for: 5 -> 13; matrix products, arithmetic and copies ran while one was open for 7% -> 12% of each run, Pallas kernels for 0% -> 0%
where the time goes in v1:
time: 81.5 us; the launch traced here: 80.7 us
  waiting for transfers between devices  34.1 us (42%)
  starting transfers between devices  33 us (40%)
  matrix products  6 us (7%)
  other arithmetic  3.67 us (5%)
  local copies, waits for them, and re-layouts  2.85 us (3%)
  between operations  1.04 us (1%)
    ppermute x9, waiting for transfers between devices, gather_by_hops(): parts = [lax.ppermute(parts[0], name, hops), *parts]  19.8 us
    ppermute x6, starting transfers between devices, from_behind(): return lax.ppermute(block, axis, route)  18.3 us
    all_to_all x3, starting transfers between devices, advance(): lax.all_to_all(down_coef, 'xy', split_axis=1, concat_axis=0, tiled=True)  9.85 us
    all_to_all x3, waiting for transfers between devices, advance(): lax.all_to_all(down_coef, 'xy', split_axis=1, concat_axis=0, tiled=True)  7.73 us
    ppermute x6, waiting for transfers between devices, from_behind(): return lax.ppermute(block, axis, route)  6.52 us
    dot_general x3, matrix products, advance(): jnp.einsum('asjb,ijcrb->ijascr', pieces, v_layer, preferred_element_type=...  3.96 us
    all_to_all x1, starting transfers between devices, on_device(): lax.all_to_all(v_layer, 'xy', split_axis=1, concat_axis=0, tiled=True)  3.47 us
    convert_element_type x3, local copies, waits for them, and re-layouts, advance(): jnp.where(keep_rank[:, :, None, None, :], down_coef, 0.0)  1.89 us
  transfers between devices with their start and end apart: 19, of which 13 were waited for; matrix products, arithmetic and copies ran while one was open for 12% of the time, Pallas kernels for 0%

profile of v1, /device:TPU:0, one launch (start us, length us, event | category | flops | bytes accessed | tf_op | source)
XLA Modules:
  0.0 80.7 jit_solution(4133404045909280844)
XLA Ops:
  0.6 0.0 copy-start
  0.7 0.7 copy-done.3
  1.4 0.8 %bitcast_select_fusion.1 = bf16[2,32,256]{2,1,0:T(8,128)(2,1)S(1)} fusion(bf16[1,2,32,256]{3,2,1,0:T(8,128)(2,1)} %param.8, pred[32]{0:T(512)(128)(4,1)S(1)} %get-tuple-element.24), kind=kLoop, calls=%fused_computation.183 | loop fusion | flops 16384 | bytes 65568 | tf_op jit(solution)/shard_map/jit(_where)/select_n | solution.py:68
  2.2 0.5 collective-permute-start
  2.7 0.1 bitcast_select_fusion
  2.8 1.3 %collective-permute-start.12 = (bf16[2,32,256]{2,1,0:T(8,128)(2,1)S(1)}, bf16[2,32,256]{2,1,0:T(8,128)(2,1)S(1)}, u32[]{:S(2)}, u32[]{:S(2)}) collective-permute-start(bf16[2,32,256]{2,1,0:T(8,128)(2,1)S(1)} %bitcast_select_fusion), channel_id=1, source_target_pairs={{4,0},{8,4},{12,8},{16,12},{20,16},{24,20},{28,24},{5,1},{9,5},{13... | collective-permute-start | bytes 98312 | tf_op jit(solution)/shard_map/ppermute | solution.py:23
  4.1 2.1 %collective-permute-done = bf16[2,32,256]{2,1,0:T(8,128)(2,1)S(1)} collective-permute-done((bf16[2,32,256]{2,1,0:T(8,128)(2,1)S(1)}, bf16[2,32,256]{2,1,0:T(8,128)(2,1)S(1)}, u32[]{:S(2)}, u32[]{:S(2)}) %collective-permute-start) | collective-permute-done | bytes 32800 | tf_op jit(solution)/shard_map/ppermute | solution.py:14
  6.2 0.5 collective-permute-start.1
  6.7 2.8 %collective-permute-done.1 = bf16[2,32,256]{2,1,0:T(8,128)(2,1)S(1)} collective-permute-done((bf16[2,32,256]{2,1,0:T(8,128)(2,1)S(1)}, bf16[2,32,256]{2,1,0:T(8,128)(2,1)S(1)}, u32[]{:S(2)}, u32[]{:S(2)}) %collective-permute-start.1) | collective-permute-done | bytes 32800 | tf_op jit(solution)/shard_map/ppermute | solution.py:14
  9.6 0.1 collective-permute-start.2
  9.7 0.1 iota_compare_fusion
  9.7 3.2 %collective-permute-done.2 = bf16[2,32,256]{2,1,0:T(8,128)(2,1)S(1)} collective-permute-done((bf16[2,32,256]{2,1,0:T(8,128)(2,1)S(1)}, bf16[2,32,256]{2,1,0:T(8,128)(2,1)S(1)}, u32[]{:S(2)}, u32[]{:S(2)}) %collective-permute-start.2) | collective-permute-done | bytes 32800 | tf_op jit(solution)/shard_map/ppermute | solution.py:14
  12.9 0.2 fusion.39
  13.1 0.1 reshape.884
  13.2 1.3 %convolution_bitcast_fusion.5 = f32[1,4,2,32,2,128]{5,3,4,2,1,0:T(8,128)S(1)} fusion(bf16[1,1,4,2,128,256]{5,4,3,2,1,0:T(8,128)(2,1)} %param.12, bf16[2,32,4,256,1]{3,2,1,0,4:T(4,128)(2,1)S(1)} %bitcast.274), kind=kOutput, calls=%fused_computation.5 | convolution fusion | flops 33554432 | bytes 917504 | tf_op jit(solution)/shard_map/asjb,ijcrb->ijascr/dot_general | solution.py:40
  14.6 0.2 convolution_bitcast_fusion.11
  14.8 0.0 copy-start.1
  14.8 4.2 %collective-permute-start.3 = (f32[2,32,256]{2,1,0:T(8,128)S(1)}, f32[2,32,256]{2,1,0:T(8,128)S(1)}, u32[]{:S(2)}, u32[]{:S(2)}) collective-permute-start(f32[2,32,256]{2,1,0:T(8,128)S(1)} %maximum_bitcast_fusion), channel_id=1, source_target_pairs={{0,4},{4,8},{8,12},{12,16},{16,20},{20,24},{24,28},{1,5},{5,9},{9,... | collective-permute-start | bytes 196616 | tf_op jit(solution)/shard_map/ppermute | solution.py:23
  19.1 0.3 convolution_bitcast_fusion.2
  19.4 1.6 %collective-permute-done.3 = f32[2,32,256]{2,1,0:T(8,128)S(1)} collective-permute-done((f32[2,32,256]{2,1,0:T(8,128)S(1)}, f32[2,32,256]{2,1,0:T(8,128)S(1)}, u32[]{:S(2)}, u32[]{:S(2)}) %collective-permute-start.3) | collective-permute-done | bytes 65568 | tf_op jit(solution)/shard_map/ppermute | solution.py:23
  21.0 0.1 fusion.54
  21.0 0.0 collective-permute-start.4
  21.1 3.3 %collective-permute-done.4 = bf16[2,32,256]{2,1,0:T(8,128)(2,1)S(1)} collective-permute-done((bf16[2,32,256]{2,1,0:T(8,128)(2,1)S(1)}, bf16[2,32,256]{2,1,0:T(8,128)(2,1)S(1)}, u32[]{:S(2)}, u32[]{:S(2)}) %collective-permute-start.4) | collective-permute-done | bytes 32800 | tf_op jit(solution)/shard_map/ppermute | solution.py:14
  24.4 3.3 %collective-permute-done.5 = bf16[2,32,256]{2,1,0:T(8,128)(2,1)S(1)} collective-permute-done((bf16[2,32,256]{2,1,0:T(8,128)(2,1)S(1)}, bf16[2,32,256]{2,1,0:T(8,128)(2,1)S(1)}, u32[]{:S(2)}, u32[]{:S(2)}) %collective-permute-start.5) | collective-permute-done | bytes 32800 | tf_op jit(solution)/shard_map/ppermute | solution.py:14
  27.7 0.6 copy.47
  28.4 3.3 %all-to-all-start = ((bf16[1,4,2,32,128]{4,3,2,0,1:T(8,128)(2,1)}), bf16[1,4,2,32,128]{4,3,2,0,1:T(8,128)(2,1)S(1)}, u32[]{:S(2)}, u32[]{:S(2)}) async-start(bf16[1,4,2,32,128]{4,3,2,0,1:T(8,128)(2,1)} %copy.47), calls=%async_computation | async-start | bytes 131072 | tf_op jit(solution)/shard_map/all_to_all | solution.py:55
  31.7 0.0 collective-permute-done.6
  31.7 0.2 fusion.32
  31.9 0.1 reshape.887
  32.0 1.3 %convolution_bitcast_fusion.4 = f32[1,4,2,32,2,128]{5,3,1,4,2,0:T(8,128)S(1)} fusion(bf16[2,32,4,256,1]{3,2,1,0,4:T(4,128)(2,1)S(1)} %bitcast.275, bf16[1,1,4,2,128,256]{5,4,3,2,1,0:T(8,128)(2,1)} %param.12), kind=kOutput, calls=%fused_computation.4 | convolution fusion | flops 33554432 | bytes 917504 | tf_op jit(solution)/shard_map/asjb,ijcrb->ijascr/dot_general | solution.py:40
  33.4 0.2 convolution_bitcast_fusion.10
  33.6 2.2 %all-to-all-done = bf16[1,4,2,32,128]{4,3,2,0,1:T(8,128)(2,1)S(1)} async-done(((bf16[1,4,2,32,128]{4,3,2,0,1:T(8,128)(2,1)}), bf16[1,4,2,32,128]{4,3,2,0,1:T(8,128)(2,1)S(1)}, u32[]{:S(2)}, u32[]{:S(2)}) %all-to-all-start) | async-done | bytes 65568 | tf_op jit(solution)/shard_map/all_to_all | solution.py:55
  35.8 3.5 %all-to-all-start.1 = ((bf16[1,4,2,128,256]{4,3,2,0,1:T(8,128)(2,1)}), bf16[1,4,2,128,256]{4,3,2,0,1:T(8,128)(2,1)S(1)}, u32[]{:S(2)}, u32[]{:S(2)}) async-start(bf16[1,4,2,128,256]{4,3,2,0,1:T(8,128)(2,1)} %bitcast.74), calls=%async_computation.1 | async-start | bytes 1048576 | tf_op jit(solution)/shard_map/all_to_all | solution.py:78
  39.2 4.3 %collective-permute-start.7 = (f32[2,32,256]{2,1,0:T(8,128)S(1)}, f32[2,32,256]{2,1,0:T(8,128)S(1)}, u32[]{:S(2)}, u32[]{:S(2)}) collective-permute-start(f32[2,32,256]{2,1,0:T(8,128)S(1)} %maximum_bitcast_fusion.1), channel_id=1, source_target_pairs={{0,4},{4,8},{8,12},{12,16},{16,20},{20,24},{24,28},{1,5},{5,9},{9,... | collective-permute-start | bytes 196616 | tf_op jit(solution)/shard_map/ppermute | solution.py:23
  43.5 1.9 %collective-permute-done.7 = f32[2,32,256]{2,1,0:T(8,128)S(1)} collective-permute-done((f32[2,32,256]{2,1,0:T(8,128)S(1)}, f32[2,32,256]{2,1,0:T(8,128)S(1)}, u32[]{:S(2)}, u32[]{:S(2)}) %collective-permute-start.7) | collective-permute-done | bytes 65568 | tf_op jit(solution)/shard_map/ppermute | solution.py:23
  45.5 0.1 fusion.55
  45.6 3.3 %collective-permute-done.8 = bf16[2,32,256]{2,1,0:T(8,128)(2,1)S(1)} collective-permute-done((bf16[2,32,256]{2,1,0:T(8,128)(2,1)S(1)}, bf16[2,32,256]{2,1,0:T(8,128)(2,1)S(1)}, u32[]{:S(2)}, u32[]{:S(2)}) %collective-permute-start.8) | collective-permute-done | bytes 32800 | tf_op jit(solution)/shard_map/ppermute | solution.py:14
  48.9 0.0 collective-permute-start.9
  48.9 0.2 convolution_bitcast_fusion.8
  49.1 0.1 fusion.52
  49.2 1.3 %collective-permute-start.13 = (bf16[2,32,256]{2,1,0:T(8,128)(2,1)S(1)}, bf16[2,32,256]{2,1,0:T(8,128)(2,1)S(1)}, u32[]{:S(2)}, u32[]{:S(2)}) collective-permute-start(bf16[2,32,256]{2,1,0:T(8,128)(2,1)S(1)} %fusion.52), channel_id=1, source_target_pairs={{4,0},{8,4},{12,8},{16,12},{20,16},{24,20},{28,24},{5,1},{9,5},{13... | collective-permute-start | bytes 98312 | tf_op jit(solution)/shard_map/ppermute | solution.py:23
  50.5 1.7 %collective-permute-done.9 = bf16[2,32,256]{2,1,0:T(8,128)(2,1)S(1)} collective-permute-done((bf16[2,32,256]{2,1,0:T(8,128)(2,1)S(1)}, bf16[2,32,256]{2,1,0:T(8,128)(2,1)S(1)}, u32[]{:S(2)}, u32[]{:S(2)}) %collective-permute-start.9) | collective-permute-done | bytes 32800 | tf_op jit(solution)/shard_map/ppermute | solution.py:14
  52.2 0.3 collective-permute-start.10
  52.6 3.0 %collective-permute-done.13 = bf16[2,32,256]{2,1,0:T(8,128)(2,1)S(1)} collective-permute-done((bf16[2,32,256]{2,1,0:T(8,128)(2,1)S(1)}, bf16[2,32,256]{2,1,0:T(8,128)(2,1)S(1)}, u32[]{:S(2)}, u32[]{:S(2)}) %collective-permute-start.13) | collective-permute-done | bytes 32800 | tf_op jit(solution)/shard_map/ppermute | solution.py:23
  55.5 0.3 convolution_bitcast_fusion.1
  55.9 0.6 copy.51
  56.5 3.3 %all-to-all-start.2 = ((bf16[1,4,2,32,128]{4,3,2,0,1:T(8,128)(2,1)}), bf16[1,4,2,32,128]{4,3,2,0,1:T(8,128)(2,1)S(1)}, u32[]{:S(2)}, u32[]{:S(2)}) async-start(bf16[1,4,2,32,128]{4,3,2,0,1:T(8,128)(2,1)} %copy.51), calls=%async_computation.2 | async-start | bytes 131072 | tf_op jit(solution)/shard_map/all_to_all | solution.py:55
  59.8 0.2 fusion.25
  60.0 0.1 reshape.888
  60.1 1.3 %convolution_bitcast_fusion.3 = f32[1,4,2,32,2,128]{5,3,1,4,2,0:T(8,128)S(1)} fusion(bf16[2,32,4,256,1]{3,2,1,0,4:T(4,128)(2,1)S(1)} %bitcast.276, bf16[1,1,4,2,128,256]{5,4,3,2,1,0:T(8,128)(2,1)} %param.12), kind=kOutput, calls=%fused_computation.3 | convolution fusion | flops 33554432 | bytes 917504 | tf_op jit(solution)/shard_map/asjb,ijcrb->ijascr/dot_general | solution.py:40
  61.5 0.2 convolution_bitcast_fusion.9
  61.7 2.2 %all-to-all-done.2 = bf16[1,4,2,32,128]{4,3,2,0,1:T(8,128)(2,1)S(1)} async-done(((bf16[1,4,2,32,128]{4,3,2,0,1:T(8,128)(2,1)}), bf16[1,4,2,32,128]{4,3,2,0,1:T(8,128)(2,1)S(1)}, u32[]{:S(2)}, u32[]{:S(2)}) %all-to-all-start.2) | async-done | bytes 65568 | tf_op jit(solution)/shard_map/all_to_all | solution.py:55
  63.9 0.2 convolution_bitcast_fusion.7
  64.1 0.1 fusion.53
  64.2 1.3 %collective-permute-start.14 = (bf16[2,32,256]{2,1,0:T(8,128)(2,1)S(1)}, bf16[2,32,256]{2,1,0:T(8,128)(2,1)S(1)}, u32[]{:S(2)}, u32[]{:S(2)}) collective-permute-start(bf16[2,32,256]{2,1,0:T(8,128)(2,1)S(1)} %fusion.53), channel_id=1, source_target_pairs={{4,0},{8,4},{12,8},{16,12},{20,16},{24,20},{28,24},{5,1},{9,5},{13... | collective-permute-start | bytes 98312 | tf_op jit(solution)/shard_map/ppermute | solution.py:23
  65.5 5.9 %collective-permute-start.11 = (f32[2,32,256]{2,1,0:T(8,128)S(1)}, f32[2,32,256]{2,1,0:T(8,128)S(1)}, u32[]{:S(2)}, u32[]{:S(2)}) collective-permute-start(f32[2,32,256]{2,1,0:T(8,128)S(1)} %maximum_bitcast_fusion.2), channel_id=1, source_target_pairs={{0,4},{4,8},{8,12},{12,16},{16,20},{20,24},{24,28},{1,5},{5,9},{9,... | collective-permute-start | bytes 196616 | tf_op jit(solution)/shard_map/ppermute | solution.py:23
  71.4 0.0 collective-permute-done.14
  71.4 0.3 convolution_bitcast_fusion
  71.8 0.6 copy.54
  72.4 3.3 %all-to-all-start.3 = ((bf16[1,4,2,32,128]{4,3,2,0,1:T(8,128)(2,1)}), bf16[1,4,2,32,128]{4,3,2,0,1:T(8,128)(2,1)S(1)}, u32[]{:S(2)}, u32[]{:S(2)}) async-start(bf16[1,4,2,32,128]{4,3,2,0,1:T(8,128)(2,1)} %copy.54), calls=%async_computation.3 | async-start | bytes 131072 | tf_op jit(solution)/shard_map/all_to_all | solution.py:55
  75.7 0.7 fusion.90
  76.4 3.4 %all-to-all-done.3 = bf16[1,4,2,32,128]{4,3,2,0,1:T(8,128)(2,1)S(1)} async-done(((bf16[1,4,2,32,128]{4,3,2,0,1:T(8,128)(2,1)}), bf16[1,4,2,32,128]{4,3,2,0,1:T(8,128)(2,1)S(1)}, u32[]{:S(2)}, u32[]{:S(2)}) %all-to-all-start.3) | async-done | bytes 65568 | tf_op jit(solution)/shard_map/all_to_all | solution.py:55
  79.8 0.2 convolution_bitcast_fusion.6
  80.0 0.7 fusion.77
  (36 shorter events, 0.3 us)
Async XLA Ops:
  0.6 13.9 %copy-start = (bf16[1,1,4,2,128,256]{5,4,3,2,1,0:T(8,128)(2,1)S(1)}, bf16[1,1,4,2,128,256]{5,4,3,2,1,0:T(8,128)(2,1)}, u32[]{:S(2)}) copy-start(bf16[1,1,4,2,128,256]{5,4,3,2,1,0:T(8,128)(2,1)} %param.11) | copy-start | bytes 1572868
  0.7 0.7 copy-start.3
  1.4 1.3 %copy-start.2 = (bf16[1,2,32,256]{3,2,1,0:T(8,128)(2,1)S(1)}, bf16[1,2,32,256]{3,2,1,0:T(8,128)(2,1)}, u32[]{:S(2)}) copy-start(bf16[1,2,32,256]{3,2,1,0:T(8,128)(2,1)} %param.9) | copy-start | bytes 98308
  2.2 4.0 %collective-permute-start = (bf16[2,32,256]{2,1,0:T(8,128)(2,1)S(1)}, bf16[2,32,256]{2,1,0:T(8,128)(2,1)S(1)}, u32[]{:S(2)}, u32[]{:S(2)}) collective-permute-start(bf16[2,32,256]{2,1,0:T(8,128)(2,1)S(1)} %bitcast_select_fusion.1), channel_id=1, source_target_pairs={{0,1},{1,2},{2,3},{3,0},{4,5},{5,6},{6,7},{7,4},{8,9},{9,10},{10,1... | collective-permute-start | bytes 98312 | tf_op jit(solution)/shard_map/ppermute | solution.py:14
  2.7 4.0 %copy-start.4 = (s32[1,1,4]{2,1,0:T(1,128)S(1)}, s32[1,1,4]{2,1,0:T(1,128)}, u32[]{:S(2)}) copy-start(s32[1,1,4]{2,1,0:T(1,128)} %param.13) | copy-start | bytes 52
  2.8 16.3 %collective-permute-start.12 = (bf16[2,32,256]{2,1,0:T(8,128)(2,1)S(1)}, bf16[2,32,256]{2,1,0:T(8,128)(2,1)S(1)}, u32[]{:S(2)}, u32[]{:S(2)}) collective-permute-start(bf16[2,32,256]{2,1,0:T(8,128)(2,1)S(1)} %bitcast_select_fusion), channel_id=1, source_target_pairs={{4,0},{8,4},{12,8},{16,12},{20,16},{24,20},{28,24},{5,1},{9,5},{13... | collective-permute-start | bytes 98312 | tf_op jit(solution)/shard_map/ppermute | solution.py:23
  6.2 3.3 %collective-permute-start.1 = (bf16[2,32,256]{2,1,0:T(8,128)(2,1)S(1)}, bf16[2,32,256]{2,1,0:T(8,128)(2,1)S(1)}, u32[]{:S(2)}, u32[]{:S(2)}) collective-permute-start(bf16[2,32,256]{2,1,0:T(8,128)(2,1)S(1)} %collective-permute-done), channel_id=1, source_target_pairs={{0,1},{1,2},{2,3},{3,0},{4,5},{5,6},{6,7},{7,4},{8,9},{9,10},{10,1... | collective-permute-start | bytes 98312 | tf_op jit(solution)/shard_map/ppermute | solution.py:14
  9.6 3.3 %collective-permute-start.2 = (bf16[2,32,256]{2,1,0:T(8,128)(2,1)S(1)}, bf16[2,32,256]{2,1,0:T(8,128)(2,1)S(1)}, u32[]{:S(2)}, u32[]{:S(2)}) collective-permute-start(bf16[2,32,256]{2,1,0:T(8,128)(2,1)S(1)} %collective-permute-done.1), channel_id=1, source_target_pairs={{0,1},{1,2},{2,3},{3,0},{4,5},{5,6},{6,7},{7,4},{8,9},{9,10},{10,1... | collective-permute-start | bytes 98312 | tf_op jit(solution)/shard_map/ppermute | solution.py:14
  14.8 6.1 %copy-start.1 = (bf16[1,2,32,256]{3,2,1,0:T(8,128)(2,1)S(1)}, bf16[1,2,32,256]{3,2,1,0:T(8,128)(2,1)}, u32[]{:S(2)}) copy-start(bf16[1,2,32,256]{3,2,1,0:T(8,128)(2,1)} %param.8) | copy-start | bytes 98308
  14.8 6.1 %collective-permute-start.3 = (f32[2,32,256]{2,1,0:T(8,128)S(1)}, f32[2,32,256]{2,1,0:T(8,128)S(1)}, u32[]{:S(2)}, u32[]{:S(2)}) collective-permute-start(f32[2,32,256]{2,1,0:T(8,128)S(1)} %maximum_bitcast_fusion), channel_id=1, source_target_pairs={{0,4},{4,8},{8,12},{12,16},{16,20},{20,24},{24,28},{1,5},{5,9},{9,... | collective-permute-start | bytes 196616 | tf_op jit(solution)/shard_map/ppermute | solution.py:23
  21.0 3.3 %collective-permute-start.4 = (bf16[2,32,256]{2,1,0:T(8,128)(2,1)S(1)}, bf16[2,32,256]{2,1,0:T(8,128)(2,1)S(1)}, u32[]{:S(2)}, u32[]{:S(2)}) collective-permute-start(bf16[2,32,256]{2,1,0:T(8,128)(2,1)S(1)} %fusion.54), channel_id=1, source_target_pairs={{0,1},{1,2},{2,3},{3,0},{4,5},{5,6},{6,7},{7,4},{8,9},{9,10},{10,1... | collective-permute-start | bytes 98312 | tf_op jit(solution)/shard_map/ppermute | solution.py:14
  24.4 3.3 %collective-permute-start.5 = (bf16[2,32,256]{2,1,0:T(8,128)(2,1)S(1)}, bf16[2,32,256]{2,1,0:T(8,128)(2,1)S(1)}, u32[]{:S(2)}, u32[]{:S(2)}) collective-permute-start(bf16[2,32,256]{2,1,0:T(8,128)(2,1)S(1)} %collective-permute-done.4), channel_id=1, source_target_pairs={{0,1},{1,2},{2,3},{3,0},{4,5},{5,6},{6,7},{7,4},{8,9},{9,10},{10,1... | collective-permute-start | bytes 98312 | tf_op jit(solution)/shard_map/ppermute | solution.py:14
  27.7 3.9 %collective-permute-start.6 = (bf16[2,32,256]{2,1,0:T(8,128)(2,1)S(1)}, bf16[2,32,256]{2,1,0:T(8,128)(2,1)S(1)}, u32[]{:S(2)}, u32[]{:S(2)}) collective-permute-start(bf16[2,32,256]{2,1,0:T(8,128)(2,1)S(1)} %collective-permute-done.5), channel_id=1, source_target_pairs={{0,1},{1,2},{2,3},{3,0},{4,5},{5,6},{6,7},{7,4},{8,9},{9,10},{10,1... | collective-permute-start | bytes 98312 | tf_op jit(solution)/shard_map/ppermute | solution.py:14
  28.4 7.4 %all-to-all-start = ((bf16[1,4,2,32,128]{4,3,2,0,1:T(8,128)(2,1)}), bf16[1,4,2,32,128]{4,3,2,0,1:T(8,128)(2,1)S(1)}, u32[]{:S(2)}, u32[]{:S(2)}) async-start(bf16[1,4,2,32,128]{4,3,2,0,1:T(8,128)(2,1)} %copy.47), calls=%async_computation | async-start | bytes 131072 | tf_op jit(solution)/shard_map/all_to_all | solution.py:55
  35.8 13.1 %all-to-all-start.1 = ((bf16[1,4,2,128,256]{4,3,2,0,1:T(8,128)(2,1)}), bf16[1,4,2,128,256]{4,3,2,0,1:T(8,128)(2,1)S(1)}, u32[]{:S(2)}, u32[]{:S(2)}) async-start(bf16[1,4,2,128,256]{4,3,2,0,1:T(8,128)(2,1)} %bitcast.74), calls=%async_computation.1 | async-start | bytes 1048576 | tf_op jit(solution)/shard_map/all_to_all | solution.py:78
  39.2 6.2 %collective-permute-start.7 = (f32[2,32,256]{2,1,0:T(8,128)S(1)}, f32[2,32,256]{2,1,0:T(8,128)S(1)}, u32[]{:S(2)}, u32[]{:S(2)}) collective-permute-start(f32[2,32,256]{2,1,0:T(8,128)S(1)} %maximum_bitcast_fusion.1), channel_id=1, source_target_pairs={{0,4},{4,8},{8,12},{12,16},{16,20},{20,24},{24,28},{1,5},{5,9},{9,... | collective-permute-start | bytes 196616 | tf_op jit(solution)/shard_map/ppermute | solution.py:23
  45.5 3.3 %collective-permute-start.8 = (bf16[2,32,256]{2,1,0:T(8,128)(2,1)S(1)}, bf16[2,32,256]{2,1,0:T(8,128)(2,1)S(1)}, u32[]{:S(2)}, u32[]{:S(2)}) collective-permute-start(bf16[2,32,256]{2,1,0:T(8,128)(2,1)S(1)} %fusion.55), channel_id=1, source_target_pairs={{0,1},{1,2},{2,3},{3,0},{4,5},{5,6},{6,7},{7,4},{8,9},{9,10},{10,1... | collective-permute-start | bytes 98312 | tf_op jit(solution)/shard_map/ppermute | solution.py:14
  48.9 3.3 %collective-permute-start.9 = (bf16[2,32,256]{2,1,0:T(8,128)(2,1)S(1)}, bf16[2,32,256]{2,1,0:T(8,128)(2,1)S(1)}, u32[]{:S(2)}, u32[]{:S(2)}) collective-permute-start(bf16[2,32,256]{2,1,0:T(8,128)(2,1)S(1)} %collective-permute-done.8), channel_id=1, source_target_pairs={{0,1},{1,2},{2,3},{3,0},{4,5},{5,6},{6,7},{7,4},{8,9},{9,10},{10,1... | collective-permute-start | bytes 98312 | tf_op jit(solution)/shard_map/ppermute | solution.py:14
  49.2 6.3 %collective-permute-start.13 = (bf16[2,32,256]{2,1,0:T(8,128)(2,1)S(1)}, bf16[2,32,256]{2,1,0:T(8,128)(2,1)S(1)}, u32[]{:S(2)}, u32[]{:S(2)}) collective-permute-start(bf16[2,32,256]{2,1,0:T(8,128)(2,1)S(1)} %fusion.52), channel_id=1, source_target_pairs={{4,0},{8,4},{12,8},{16,12},{20,16},{24,20},{28,24},{5,1},{9,5},{13... | collective-permute-start | bytes 98312 | tf_op jit(solution)/shard_map/ppermute | solution.py:23
  52.2 7.6 %collective-permute-start.10 = (bf16[2,32,256]{2,1,0:T(8,128)(2,1)S(1)}, bf16[2,32,256]{2,1,0:T(8,128)(2,1)S(1)}, u32[]{:S(2)}, u32[]{:S(2)}) collective-permute-start(bf16[2,32,256]{2,1,0:T(8,128)(2,1)S(1)} %collective-permute-done.9), channel_id=1, source_target_pairs={{0,1},{1,2},{2,3},{3,0},{4,5},{5,6},{6,7},{7,4},{8,9},{9,10},{10,1... | collective-permute-start | bytes 98312 | tf_op jit(solution)/shard_map/ppermute | solution.py:14
  56.5 7.4 %all-to-all-start.2 = ((bf16[1,4,2,32,128]{4,3,2,0,1:T(8,128)(2,1)}), bf16[1,4,2,32,128]{4,3,2,0,1:T(8,128)(2,1)S(1)}, u32[]{:S(2)}, u32[]{:S(2)}) async-start(bf16[1,4,2,32,128]{4,3,2,0,1:T(8,128)(2,1)} %copy.51), calls=%async_computation.2 | async-start | bytes 131072 | tf_op jit(solution)/shard_map/all_to_all | solution.py:55
  64.2 7.2 %collective-permute-start.14 = (bf16[2,32,256]{2,1,0:T(8,128)(2,1)S(1)}, bf16[2,32,256]{2,1,0:T(8,128)(2,1)S(1)}, u32[]{:S(2)}, u32[]{:S(2)}) collective-permute-start(bf16[2,32,256]{2,1,0:T(8,128)(2,1)S(1)} %fusion.53), channel_id=1, source_target_pairs={{4,0},{8,4},{12,8},{16,12},{20,16},{24,20},{28,24},{5,1},{9,5},{13... | collective-permute-start | bytes 98312 | tf_op jit(solution)/shard_map/ppermute | solution.py:23
  65.5 10.2 %collective-permute-start.11 = (f32[2,32,256]{2,1,0:T(8,128)S(1)}, f32[2,32,256]{2,1,0:T(8,128)S(1)}, u32[]{:S(2)}, u32[]{:S(2)}) collective-permute-start(f32[2,32,256]{2,1,0:T(8,128)S(1)} %maximum_bitcast_fusion.2), channel_id=1, source_target_pairs={{0,4},{4,8},{8,12},{12,16},{16,20},{20,24},{24,28},{1,5},{5,9},{9,... | collective-permute-start | bytes 196616 | tf_op jit(solution)/shard_map/ppermute | solution.py:23
  72.4 7.4 %all-to-all-start.3 = ((bf16[1,4,2,32,128]{4,3,2,0,1:T(8,128)(2,1)}), bf16[1,4,2,32,128]{4,3,2,0,1:T(8,128)(2,1)S(1)}, u32[]{:S(2)}, u32[]{:S(2)}) async-start(bf16[1,4,2,32,128]{4,3,2,0,1:T(8,128)(2,1)} %copy.54), calls=%async_computation.3 | async-start | bytes 131072 | tf_op jit(solution)/shard_map/all_to_all | solution.py:55
